TPU v7x, 32 devices: a whole 2x2x4 slice. The times are simulated.
32 devices in a mesh: seq: 16 (over z, y, core), mp: 2 (over x).
Axes of the slice: x: 2, y: 2, z: 4, core: 2. Of those that a mesh axis runs over, the one named last changes fastest.
Arguments:
- shared_qk: bfloat16 [2048, 4096], P('seq', 'mp'), may hold values from -40 to 40
- values: bfloat16 [2048, 4096], P('seq', 'mp'), may hold values from -6 to 6
- buckets: int32 [2048, 32], P('seq', 'mp'), may hold values from 0 to 15, as said below
- counts: int32 [16, 32, 16], P(None, 'mp'), may hold values from 0 to 16, as said below
- w_out: bfloat16 [4096, 4096], P('mp'), may hold values from -0.09375 to 0.09375
Outputs:
- projected: bfloat16 [2048, 4096], P('seq', 'mp')
Inputs may be any that keep to these rules, and one draw needn't show every extreme that they name: `buckets`: in each head at most 16 tokens among rows d * 128 to (d + 1) * 128 - 1 name one bucket, and in each head one bucket is named by exactly 16 tokens of every such group of rows. counts[d, h, b] is the number of rows among d * 128 to (d + 1) * 128 - 1 whose bucket in head h is b.
All inputs are finite; a program needn't handle non-finite values.
Results may differ from a plain program's by a relative error of at most 0.0057.
Values may be sent and summed in bfloat16 or wider, within the bound.
No kernel may reach another device: no remote copies, remote signals or barrier semaphores. Data moves between devices by JAX's collectives and lax.ppermute only.
A program may use at most 64 MiB of HBM per device.

v0:
```python
import math
import jax
import jax.numpy as jnp
from jax import lax
from jax.sharding import PartitionSpec as P

BLOCK = 256
SELF_SCORE = -100000.0


def passed_along(shard, axis, by):
    devices = lax.axis_size(axis)
    return lax.ppermute(shard, axis, [(i, (i + by) % devices) for i in range(devices)])


def block_attention(queries, window, window_live):
    head_dim = queries.shape[-1]
    block_rows = queries.shape[-2]
    key_rows = window[..., :head_dim]
    value_rows = window[..., head_dim:]
    scores = jnp.einsum("cqd,ckd->cqk", queries, key_rows, preferred_element_type=jnp.float32) * (
        1.0 / math.sqrt(head_dim)
    )
    query_place = jnp.arange(block_rows)[:, None] + block_rows
    key_place = jnp.arange(2 * block_rows)[None, :]
    itself = query_place == key_place
    scores = jnp.where(itself[None], SELF_SCORE, scores)
    allowed = window_live[:, None, :] | itself[None]
    row_max = jnp.max(jnp.where(allowed, scores, -1e30), axis=-1, keepdims=True)
    exp_terms = jnp.where(allowed, jnp.exp(scores - row_max), 0.0)
    weights = (exp_terms / jnp.sum(exp_terms, axis=-1, keepdims=True)).astype(jnp.bfloat16)
    attended = jnp.einsum("cqk,ckd->cqd", weights, value_rows, preferred_element_type=jnp.float32)
    return attended.astype(jnp.bfloat16)


def owner_layout(received, column, slot_count):
    source_count = column.shape[0]
    head_count = column.shape[1]
    upto_count = jnp.cumsum(column, axis=0)
    before_count = upto_count - column
    bucket_total = upto_count[-1]
    slot_range = jnp.arange(slot_count)
    source_dev = jnp.sum(upto_count[:, :, None] <= slot_range[None, None, :], axis=0)
    source_dev = jnp.minimum(source_dev, source_count - 1)
    source_range = jnp.arange(source_count)
    source_start = jnp.sum(
        jnp.where(source_dev[None] == source_range[:, None, None], before_count[:, :, None], 0),
        axis=0,
    )
    entry_row = jnp.clip(slot_range[None, :] - source_start, 0, received.shape[2] - 1)
    head_range = jnp.arange(head_count)
    layout = received[source_dev, head_range[:, None], entry_row]
    live = slot_range[None, :] < bucket_total[:, None]
    layout = jnp.where(live[..., None], layout, jnp.zeros((), layout.dtype))
    return (layout, live, before_count, bucket_total)


def tail_live(bucket_total, block_rows):
    return bucket_total[:, None] - block_rows + jnp.arange(block_rows)[None, :] >= 0


def last_rows(layout, bucket_total, block_rows):
    rank_index = bucket_total[:, None] - block_rows + jnp.arange(block_rows)[None, :]
    head_range = jnp.arange(layout.shape[0])
    rows = layout[head_range[:, None], jnp.maximum(rank_index, 0)]
    return jnp.where((rank_index >= 0)[..., None], rows, jnp.zeros((), rows.dtype))


def local(shared_qk, values, buckets, counts, w_out):
    tok_rows = shared_qk.shape[0]
    head_count = buckets.shape[1]
    head_dim = shared_qk.shape[1] // head_count
    seq_count = lax.axis_size("seq")
    capacity = 2 * tok_rows // seq_count
    slot_count = seq_count * capacity
    block_rows = BLOCK
    block_count = slot_count // block_rows
    own_index = lax.axis_index("seq")
    prev_index = (own_index + seq_count - 1) % seq_count
    head_range = jnp.arange(head_count)
    bucket_heads = buckets.T
    positions = jnp.arange(tok_rows)
    earlier = positions[None, :] < positions[:, None]
    same_bucket = bucket_heads[:, :, None] == bucket_heads[:, None, :]
    within = jnp.sum(same_bucket & earlier[None], axis=2)
    own_counts = lax.dynamic_index_in_dim(counts, own_index, 0, keepdims=False)
    own_starts = jnp.cumsum(own_counts, axis=1) - own_counts
    bucket_range = jnp.arange(seq_count)
    one_hot = bucket_heads[:, :, None] == bucket_range[None, None, :]
    token_start = jnp.sum(jnp.where(one_hot, own_starts[:, None, :], 0), axis=2)
    sorted_pos = token_start + within
    token_order = jnp.sum(
        jnp.where(sorted_pos[:, :, None] == positions[None, None, :], positions[None, :, None], 0),
        axis=1,
    )
    slot_range = jnp.arange(capacity)
    send_index = own_starts.T[:, :, None] + slot_range[None, None, :]
    filled = slot_range[None, None, :] < own_counts.T[:, :, None]
    token_pick = token_order[head_range[None, :, None], jnp.minimum(send_index, tok_rows - 1)]
    packed = jnp.concatenate(
        [
            shared_qk.reshape(tok_rows, head_count, head_dim),
            values.reshape(tok_rows, head_count, head_dim),
        ],
        axis=2,
    )
    outgoing = packed[token_pick, head_range[None, :, None]]
    outgoing = jnp.where(filled[..., None], outgoing, jnp.zeros((), outgoing.dtype))
    own_column = lax.dynamic_index_in_dim(counts, own_index, 2, keepdims=False)
    prev_column = lax.dynamic_index_in_dim(counts, prev_index, 2, keepdims=False)
    prev_total = jnp.sum(prev_column, axis=0)
    received = lax.all_to_all(outgoing, "seq", split_axis=0, concat_axis=0, tiled=True)
    layout, live, before_count, bucket_total = owner_layout(received, own_column, slot_count)
    tail_rows = last_rows(layout, bucket_total, block_rows)
    prev_rows = passed_along(tail_rows, "seq", 1)
    prev_live = tail_live(prev_total, block_rows)
    keys_all = jnp.concatenate([prev_rows, layout], axis=1)
    live_all = jnp.concatenate([prev_live, live], axis=1)
    window = jnp.concatenate(
        [
            keys_all[:, :slot_count].reshape(head_count, block_count, block_rows, 2 * head_dim),
            keys_all[:, block_rows:].reshape(head_count, block_count, block_rows, 2 * head_dim),
        ],
        axis=2,
    )
    window_live = jnp.concatenate(
        [
            live_all[:, :slot_count].reshape(head_count, block_count, block_rows),
            live_all[:, block_rows:].reshape(head_count, block_count, block_rows),
        ],
        axis=2,
    )
    queries = layout[..., :head_dim].reshape(head_count, block_count, block_rows, head_dim)
    attended = lax.map(
        lambda per_head: block_attention(per_head[0], per_head[1], per_head[2]),
        (queries, window, window_live),
    )
    out_layout = attended.reshape(head_count, slot_count, head_dim)
    back_index = before_count[:, :, None] + slot_range[None, None, :]
    back_filled = slot_range[None, None, :] < own_column[:, :, None]
    back_rows = out_layout[head_range[None, :, None], jnp.minimum(back_index, slot_count - 1)]
    back_rows = jnp.where(back_filled[..., None], back_rows, jnp.zeros((), back_rows.dtype))
    returned = lax.all_to_all(back_rows, "seq", split_axis=0, concat_axis=0, tiled=True)
    token_out = returned[buckets, head_range[None, :], within.T]
    token_out = token_out.reshape(tok_rows, head_count * head_dim)
    partial_sum = jnp.dot(token_out, w_out, preferred_element_type=jnp.float32)
    projected = lax.psum_scatter(partial_sum, "mp", scatter_dimension=1, tiled=True)
    return projected.astype(jnp.bfloat16)


def solution(mesh):
    placed = (P("seq", "mp"), P("seq", "mp"), P("seq", "mp"), P(None, "mp", None), P("mp", None))
    return jax.shard_map(
        local, mesh=mesh, in_specs=placed, out_specs=P("seq", "mp"), check_vma=False
    )
```

profile of v0, /device:TPU:0, one launch (start us, length us, event | category | flops | bytes accessed | tf_op | source)
XLA Modules:
  0.0 400.5 jit_solution(6937091656879628295)
XLA Ops:
  8.3 1.4 convert_reduce_fusion
  10.4 25.6 %gather_fusion = s32[4096]{0:T(1024)S(1)} fusion(s32[16,128]{1,0:T(8,128)S(1)} %select_reduce_fusion.1, s32[4096]{0:T(1024)S(1)} %reshape.373), kind=kCustom, calls=%fused_computation | custom fusion | bytes 65536 | tf_op jit(solution)/shard_map/gather | solution.py:99
  36.8 21.6 %gather_fusion.1 = bf16[4096,256]{1,0:T(8,128)(2,1)S(1)} fusion(bf16[128,16,256]{2,1,0:T(8,128)(2,1)S(1)} %pad_maximum_fusion, s32[4096]{0:T(1024)S(1)} %reshape.379), kind=kCustom, calls=%fused_computation.1 | custom fusion | bytes 4227072 | tf_op jit(solution)/shard_map/gather | solution.py:107
  58.4 1.7 broadcast_select_fusion.2
  60.1 7.5 %all-to-all-start = ((bf16[16,16,16,256]{3,2,1,0:T(8,128)(2,1)}), bf16[16,16,16,256]{3,2,1,0:T(8,128)(2,1)S(1)}, u32[]{:S(2)}, u32[]{:S(2)}) async-start(bf16[16,16,16,256]{3,2,1,0:T(8,128)(2,1)} %broadcast_select_fusion.2), calls=%async_computation | async-start | bytes 4194304 | tf_op jit(solution)/shard_map/all_to_all | solution.py:112
  68.7 40.0 %all-to-all-done = bf16[16,16,16,256]{3,2,1,0:T(8,128)(2,1)S(1)} async-done(((bf16[16,16,16,256]{3,2,1,0:T(8,128)(2,1)}), bf16[16,16,16,256]{3,2,1,0:T(8,128)(2,1)S(1)}, u32[]{:S(2)}, u32[]{:S(2)}) %all-to-all-start) | async-done | bytes 2097184 | tf_op jit(solution)/shard_map/all_to_all | solution.py:112
  108.7 45.3 %gather_fusion.2 = bf16[4096,256]{1,0:T(8,128)(2,1)} fusion(bf16[16,16,16,256]{3,2,1,0:T(8,128)(2,1)S(1)} %all-to-all-done, s32[4096]{0:T(1024)S(1)} %bitcast.112), kind=kCustom, calls=%fused_computation.2 | custom fusion | bytes 4243456 | tf_op jit(solution)/shard_map/gather | solution.py:52
  154.0 1.9 broadcast_select_fusion.3
  155.9 40.7 %gather_fusion.3 = bf16[4096,256]{1,0:T(8,128)(2,1)} fusion(bf16[16,256,256]{2,1,0:T(8,128)(2,1)S(1)} %broadcast_select_fusion.3, s32[4096]{0:T(1024)S(1)} %bitcast.113), kind=kCustom, calls=%fused_computation.3 | custom fusion | bytes 4227072 | tf_op jit(solution)/shard_map/gather | solution.py:65
  196.6 2.9 broadcast_select_fusion.1
  203.6 29.9 %collective-permute-done = bf16[16,256,256]{2,1,0:T(8,128)(2,1)} collective-permute-done((bf16[16,256,256]{2,1,0:T(8,128)(2,1)}, bf16[16,256,256]{2,1,0:T(8,128)(2,1)}, u32[]{:S(2)}, u32[]{:S(2)}) %collective-permute-start) | collective-permute-done | bytes 2097184 | tf_op jit(solution)/shard_map/ppermute | solution.py:13
  233.4 3.9 maximum_bitcast_fusion
  237.3 47.1 %while.10 = (s32[]{:T(128)}, bf16[16,1,256,128]{3,2,1,0:T(8,128)(2,1)S(1)}, pred[16,1,512]{2,0,1:T(8,128)(4,1)S(1)}, bf16[16,1,256,128]{3,2,1,0:T(8,128)(2,1)}, bf16[16,1,512,256]{3,2,1,0:T(8,128)(2,1)}, /*index=5*/s32[]{:T(128)}) while((s32[]{:T(128)}, bf16[16,1,256,128]{3,2,1,0:T(8,128)(2,1)S(1)}, pred[16,1,512]{2,0,1:T(8,128)(4,1)S(1)}, ...), condition=%wide.region_11.12_spmd, body=%wide.region_8.11_spmd.sunk | while | flops 69369600 | bytes 2502737 | solution.py:134
  238.3 1.2 select_reduce_fusion.5
  241.3 1.2 select_reduce_fusion.5
  247.1 1.2 select_reduce_fusion.5
  250.1 1.2 select_reduce_fusion.5
  253.0 1.2 select_reduce_fusion.5
  256.0 1.2 select_reduce_fusion.5
  258.9 1.2 select_reduce_fusion.5
  264.8 1.2 select_reduce_fusion.5
  270.7 1.2 select_reduce_fusion.5
  276.6 1.2 select_reduce_fusion.5
  282.5 1.2 select_reduce_fusion.5
  284.4 21.7 %gather_fusion.4 = bf16[4096,128]{1,0:T(8,128)(2,1)S(1)} fusion(bf16[16,256,128]{2,1,0:T(8,128)(2,1)S(1)} %bitcast.114, s32[4096]{0:T(1024)S(1)} %reshape.397), kind=kCustom, calls=%fused_computation.4 | custom fusion | bytes 2129920 | tf_op jit(solution)/shard_map/gather | solution.py:141
  306.2 1.5 broadcast_select_fusion.4
  307.7 3.7 all-to-all-start.1
  311.8 22.4 %all-to-all-done.1 = bf16[16,16,16,128]{3,2,1,0:T(8,128)(2,1)S(1)} async-done(((bf16[16,16,16,128]{3,2,1,0:T(8,128)(2,1)}), bf16[16,16,16,128]{3,2,1,0:T(8,128)(2,1)S(1)}, u32[]{:S(2)}, u32[]{:S(2)}) %all-to-all-start.1) | async-done | bytes 1048608 | tf_op jit(solution)/shard_map/all_to_all | solution.py:143
  334.2 13.4 %gather_fusion.5 = bf16[2048,128]{1,0:T(8,128)(2,1)S(1)} fusion(bf16[16,16,16,128]{3,2,1,0:T(8,128)(2,1)S(1)} %all-to-all-done.1, s32[2048]{0:T(1024)S(1)} %reshape.403), kind=kCustom, calls=%fused_computation.5 | custom fusion | bytes 1073152 | tf_op jit(solution)/shard_map/gather | solution.py:144
  347.8 9.5 %fusion.41 = f32[128,4096]{1,0:T(8,128)} fusion(bf16[128,2048]{1,0:T(8,128)(2,1)S(1)} %reshape.372, bf16[2048,4096]{1,0:T(8,128)(2,1)} %param.11), kind=kOutput, calls=%fused_computation.103 | convolution fusion | flops 2147483648 | bytes 19398656 | tf_op jit(solution)/shard_map/dot_general | solution.py:146
  357.3 34.2 %reduce-scatter.2.cloned.1.call-done = f32[128,2048]{1,0:T(8,128)} async-done(((f32[128,4096]{1,0:T(8,128)}), f32[128,2048]{1,0:T(8,128)}) %reduce-scatter.2.cloned.1.call-update) | async-done | bytes 1048592 | tf_op jit(solution)/shard_map/reduce_scatter | solution.py:147
  391.5 2.1 convert_element_type.19
  (144 shorter events, 42.1 us)
Async XLA Ops:
  10.3 25.9 %copy-start.2 = (bf16[128,2048]{1,0:T(8,128)(2,1)S(1)}, bf16[128,2048]{1,0:T(8,128)(2,1)}, u32[]{:S(2)}) copy-start(bf16[128,2048]{1,0:T(8,128)(2,1)} %param.7) | copy-start | bytes 1572868
  10.3 26.0 %copy-start.3 = (bf16[128,2048]{1,0:T(8,128)(2,1)S(1)}, bf16[128,2048]{1,0:T(8,128)(2,1)}, u32[]{:S(2)}) copy-start(bf16[128,2048]{1,0:T(8,128)(2,1)} %param.8) | copy-start | bytes 1572868
  60.1 7.6 %copy-start.1 = (s32[16,16,16]{2,1,0:T(8,128)S(1)}, s32[16,16,16]{2,1,0:T(8,128)}, u32[]{:S(2)}) copy-start(s32[16,16,16]{2,1,0:T(8,128)} %param.10) | copy-start | bytes 49156
  60.1 48.5 %all-to-all-start = ((bf16[16,16,16,256]{3,2,1,0:T(8,128)(2,1)}), bf16[16,16,16,256]{3,2,1,0:T(8,128)(2,1)S(1)}, u32[]{:S(2)}, u32[]{:S(2)}) async-start(bf16[16,16,16,256]{3,2,1,0:T(8,128)(2,1)} %broadcast_select_fusion.2), calls=%async_computation | async-start | bytes 4194304 | tf_op jit(solution)/shard_map/all_to_all | solution.py:112
  199.5 33.9 %collective-permute-start = (bf16[16,256,256]{2,1,0:T(8,128)(2,1)}, bf16[16,256,256]{2,1,0:T(8,128)(2,1)}, u32[]{:S(2)}, u32[]{:S(2)}) collective-permute-start(bf16[16,256,256]{2,1,0:T(8,128)(2,1)} %broadcast_select_fusion.1), channel_id=1, source_target_pairs={{0,2},{2,4},{4,6},{6,8},{8,10},{10,12},{12,14},{14,16},{16,18},{18... | collective-permute-start | bytes 6291464 | tf_op jit(solution)/shard_map/ppermute | solution.py:13
  200.7 2.0 copy-start
  306.2 5.4 %copy-start.4 = (s32[128,16]{0,1:T(8,128)S(1)}, s32[128,16]{0,1:T(8,128)}, u32[]{:S(2)}) copy-start(s32[128,16]{0,1:T(8,128)} %param.9) | copy-start | bytes 24580
  307.7 26.5 %all-to-all-start.1 = ((bf16[16,16,16,128]{3,2,1,0:T(8,128)(2,1)}), bf16[16,16,16,128]{3,2,1,0:T(8,128)(2,1)S(1)}, u32[]{:S(2)}, u32[]{:S(2)}) async-start(bf16[16,16,16,128]{3,2,1,0:T(8,128)(2,1)} %broadcast_select_fusion.4), calls=%async_computation.1 | async-start | bytes 2097152 | tf_op jit(solution)/shard_map/all_to_all | solution.py:143
  311.4 80.2 %reduce-scatter.2.cloned.1.call-start = ((), (), s32[]{:S(2)}) async-start(), calls=%async_computation.3 | async-start | bytes 3145728 | tf_op jit(solution)/shard_map/reduce_scatter | solution.py:147
Sparse Core Ops, SparseCore 0:
  357.5 34.0 reduce-scatter.1
where the time goes:
time: 402 us; the launch traced here: 400 us
  local copies, waits for them, and re-layouts  188 us (47%)
  waiting for transfers between devices  126 us (31%)
  matrix products  35 us (9%)
  other arithmetic  24.3 us (6%)
  between operations  13.8 us (3%)
  starting transfers between devices  12.4 us (3%)
    gather x1, local copies, waits for them, and re-layouts, owner_layout(): layout = received[source_dev, head_range[:, None], entry_row]  45.3 us
    gather x1, local copies, waits for them, and re-layouts, last_rows(): rows = layout[head_range[:, None], jnp.maximum(rank_index, 0)]  40.7 us
    all_to_all x1, waiting for transfers between devices, local(): lax.all_to_all(outgoing, 'seq', split_axis=0, concat_axis=0, tiled=True)  40 us
    reduce_scatter x1, waiting for transfers between devices, local(): lax.psum_scatter(partial_sum, 'mp', scatter_dimension=1, tiled=True)  34.2 us
    ppermute x1, waiting for transfers between devices, passed_along(): lax.ppermute(shard, axis, [(i, (i + by) % devices) for i in range(devices)])  29.9 us
    gather x2, local copies, waits for them, and re-layouts, local(): token_order[head_range[None, :, None], jnp.minimum(send_index, tok_rows -...  25.7 us
    all_to_all x1, waiting for transfers between devices, local(): lax.all_to_all(back_rows, 'seq', split_axis=0, concat_axis=0, tiled=True)  22.4 us
    gather x1, local copies, waits for them, and re-layouts, local(): out_layout[head_range[None, :, None], jnp.minimum(back_index, slot_count...  21.7 us
  transfers between devices with their start and end apart: 4, of which 4 were waited for; matrix products, arithmetic and copies ran while one was open for 1% of the time, Pallas kernels for 0%

commit v1 on v0

--- a/solution.py
+++ b/solution.py
@@ -6,6 +6,17 @@
 
 BLOCK = 256
 SELF_SCORE = -100000.0
+
+
+def in_blocks(x, dim, devices):
+    before, after = (x.shape[:dim], x.shape[dim + 1 :])
+    return jnp.moveaxis(x.reshape(*before, devices, -1, *after), dim, 0)
+
+
+def joined_along(blocks, dim):
+    blocks = jnp.moveaxis(blocks, 0, dim)
+    lengths = blocks.shape
+    return blocks.reshape(*lengths[:dim], lengths[dim] * lengths[dim + 1], *lengths[dim + 2 :])
 
 
 def passed_along(shard, axis, by):
@@ -140,7 +151,16 @@
     back_filled = slot_range[None, None, :] < own_column[:, :, None]
     back_rows = out_layout[head_range[None, :, None], jnp.minimum(back_index, slot_count - 1)]
     back_rows = jnp.where(back_filled[..., None], back_rows, jnp.zeros((), back_rows.dtype))
-    returned = lax.all_to_all(back_rows, "seq", split_axis=0, concat_axis=0, tiled=True)
+    devices_2, position = (lax.axis_size("seq"), lax.axis_index("seq"))
+    parts = in_blocks(back_rows, 0, devices_2)
+    outs = [parts[position]]
+    for lap in range(1, devices_2):
+        sent = parts[(position + lap) % devices_2]
+        outs.append(
+            lax.ppermute(sent, "seq", [(i_2, (i_2 + lap) % devices_2) for i_2 in range(devices_2)])
+        )
+    parts = jnp.stack(outs)[(position - jnp.arange(devices_2)) % devices_2]
+    returned = joined_along(parts, 0)
     token_out = returned[buckets, head_range[None, :], within.T]
     token_out = token_out.reshape(tok_rows, head_count * head_dim)
     partial_sum = jnp.dot(token_out, w_out, preferred_element_type=jnp.float32)

time: 402 us -> 426 us (1.060)
  local copies, waits for them, and re-layouts: 188 us -> 208 us
  starting transfers between devices: 12.4 us -> 25.5 us
  waiting for transfers between devices: 126 us -> 116 us
    all_to_all x1 -> x0, waiting for transfers between devices: 22.4 us -> none  [local(): lax.all_to_all(back_rows, 'seq', split_axis=0, concat_axis=0, tiled=True)]
    gather x1, local copies, waits for them, and re-layouts: 21.6 us -> 40.7 us  [local(): outgoing = packed[token_pick, head_range[None, :, None]]]
    ppermute x0 -> x15, starting transfers between devices: none -> 17 us  [local(): lax.ppermute(sent, 'seq', [(i_2, (i_2 + lap) % devices_2) for i_2 in rang...]
    ppermute x0 -> x15, waiting for transfers between devices: none -> 12.8 us  [local(): lax.ppermute(sent, 'seq', [(i_2, (i_2 + lap) % devices_2) for i_2 in rang...]
  transfers between devices with their start and end apart: 4 -> 18, of which waited for: 4 -> 9; matrix products, arithmetic and copies ran while one was open for 1% -> 1% of each run, Pallas kernels for 0% -> 0%
where the time goes in v1:
time: 426 us; the launch traced here: 424 us
  local copies, waits for them, and re-layouts  208 us (49%)
  waiting for transfers between devices  116 us (27%)
  matrix products  35 us (8%)
  starting transfers between devices  25.5 us (6%)
  other arithmetic  24.7 us (6%)
  between operations  13.9 us (3%)
    gather x1, local copies, waits for them, and re-layouts, owner_layout(): layout = received[source_dev, head_range[:, None], entry_row]  45.3 us
    gather x1, local copies, waits for them, and re-layouts, local(): outgoing = packed[token_pick, head_range[None, :, None]]  40.7 us
    gather x1, local copies, waits for them, and re-layouts, last_rows(): rows = layout[head_range[:, None], jnp.maximum(rank_index, 0)]  40.7 us
    all_to_all x1, waiting for transfers between devices, local(): lax.all_to_all(outgoing, 'seq', split_axis=0, concat_axis=0, tiled=True)  39.9 us
    reduce_scatter x1, waiting for transfers between devices, local(): lax.psum_scatter(partial_sum, 'mp', scatter_dimension=1, tiled=True)  33.4 us
    ppermute x1, waiting for transfers between devices, passed_along(): lax.ppermute(shard, axis, [(i, (i + by) % devices) for i in range(devices)])  29.6 us
    gather x2, local copies, waits for them, and re-layouts, local(): token_order[head_range[None, :, None], jnp.minimum(send_index, tok_rows -...  25.7 us
    gather x1, local copies, waits for them, and re-layouts, local(): out_layout[head_range[None, :, None], jnp.minimum(back_index, slot_count...  21.7 us
  transfers between devices with their start and end apart: 18, of which 9 were waited for; matrix products, arithmetic and copies ran while one was open for 1% of the time, Pallas kernels for 0%

profile of v1, /device:TPU:0, one launch (start us, length us, event | category | flops | bytes accessed | tf_op | source)
XLA Modules:
  0.0 423.7 jit_solution(9318320866908785657)
XLA Ops:
  8.3 1.4 convert_reduce_fusion
  10.4 25.6 %gather_fusion = s32[4096]{0:T(1024)S(1)} fusion(s32[16,128]{1,0:T(8,128)S(1)} %select_reduce_fusion.1, s32[4096]{0:T(1024)S(1)} %reshape.458), kind=kCustom, calls=%fused_computation | custom fusion | bytes 65536 | tf_op jit(solution)/shard_map/gather | solution.py:110
  36.8 40.7 %gather_fusion.1 = bf16[4096,256]{1,0:T(8,128)(2,1)} fusion(bf16[128,16,256]{2,1,0:T(8,128)(2,1)S(1)} %pad_maximum_fusion, s32[4096]{0:T(1024)S(1)} %reshape.464), kind=kCustom, calls=%fused_computation.1 | custom fusion | bytes 4227072 | tf_op jit(solution)/shard_map/gather | solution.py:118
  77.5 2.9 broadcast_select_fusion.2
  80.4 7.5 %all-to-all-start = ((bf16[16,16,16,256]{3,2,1,0:T(8,128)(2,1)}), bf16[16,16,16,256]{3,2,1,0:T(8,128)(2,1)S(1)}, u32[]{:S(2)}, u32[]{:S(2)}) async-start(bf16[16,16,16,256]{3,2,1,0:T(8,128)(2,1)} %broadcast_select_fusion.2), calls=%async_computation | async-start | bytes 4194304 | tf_op jit(solution)/shard_map/all_to_all | solution.py:123
  89.0 39.9 %all-to-all-done = bf16[16,16,16,256]{3,2,1,0:T(8,128)(2,1)S(1)} async-done(((bf16[16,16,16,256]{3,2,1,0:T(8,128)(2,1)}), bf16[16,16,16,256]{3,2,1,0:T(8,128)(2,1)S(1)}, u32[]{:S(2)}, u32[]{:S(2)}) %all-to-all-start) | async-done | bytes 2097184 | tf_op jit(solution)/shard_map/all_to_all | solution.py:123
  128.9 45.3 %gather_fusion.2 = bf16[4096,256]{1,0:T(8,128)(2,1)} fusion(bf16[16,16,16,256]{3,2,1,0:T(8,128)(2,1)S(1)} %all-to-all-done, s32[4096]{0:T(1024)S(1)} %bitcast.147), kind=kCustom, calls=%fused_computation.2 | custom fusion | bytes 4243456 | tf_op jit(solution)/shard_map/gather | solution.py:63
  174.3 1.9 broadcast_select_fusion.3
  176.2 40.7 %gather_fusion.3 = bf16[4096,256]{1,0:T(8,128)(2,1)} fusion(bf16[16,256,256]{2,1,0:T(8,128)(2,1)S(1)} %broadcast_select_fusion.3, s32[4096]{0:T(1024)S(1)} %bitcast.148), kind=kCustom, calls=%fused_computation.3 | custom fusion | bytes 4227072 | tf_op jit(solution)/shard_map/gather | solution.py:76
  216.9 2.9 broadcast_select_fusion.1
  224.1 29.6 %collective-permute-done = bf16[16,256,256]{2,1,0:T(8,128)(2,1)} collective-permute-done((bf16[16,256,256]{2,1,0:T(8,128)(2,1)}, bf16[16,256,256]{2,1,0:T(8,128)(2,1)}, u32[]{:S(2)}, u32[]{:S(2)}) %collective-permute-start) | collective-permute-done | bytes 2097184 | tf_op jit(solution)/shard_map/ppermute | solution.py:24
  253.7 3.9 maximum_bitcast_fusion
  257.6 47.1 %while.10 = (s32[]{:T(128)}, bf16[16,1,256,128]{3,2,1,0:T(8,128)(2,1)S(1)}, pred[16,1,512]{2,0,1:T(8,128)(4,1)S(1)}, bf16[16,1,256,128]{3,2,1,0:T(8,128)(2,1)}, bf16[16,1,512,256]{3,2,1,0:T(8,128)(2,1)}, /*index=5*/s32[]{:T(128)}) while((s32[]{:T(128)}, bf16[16,1,256,128]{3,2,1,0:T(8,128)(2,1)S(1)}, pred[16,1,512]{2,0,1:T(8,128)(4,1)S(1)}, ...), condition=%wide.region_11.12_spmd, body=%wide.region_8.11_spmd.sunk | while | flops 69369600 | bytes 2502737 | solution.py:145
  258.6 1.2 select_reduce_fusion.5
  264.5 1.2 select_reduce_fusion.5
  270.4 1.2 select_reduce_fusion.5
  276.3 1.2 select_reduce_fusion.5
  294.0 1.2 select_reduce_fusion.5
  304.7 21.7 %gather_fusion.4 = bf16[4096,128]{1,0:T(8,128)(2,1)S(1)} fusion(bf16[16,256,128]{2,1,0:T(8,128)(2,1)S(1)} %bitcast.149, s32[4096]{0:T(1024)S(1)} %reshape.482), kind=kCustom, calls=%fused_computation.4 | custom fusion | bytes 2129920 | tf_op jit(solution)/shard_map/gather | solution.py:152
  327.6 2.3 collective-permute-start.3
  329.9 1.7 collective-permute-start.4
  331.5 2.4 collective-permute-done.1
  335.2 1.8 collective-permute-start.7
  337.8 1.4 collective-permute-start.9
  339.2 6.5 %collective-permute-done.5 = bf16[1,16,16,128]{3,2,1,0:T(8,128)(2,1)S(1)} collective-permute-done((bf16[1,16,16,128]{3,2,1,0:T(8,128)(2,1)S(1)}, bf16[1,16,16,128]{3,2,1,0:T(8,128)(2,1)S(1)}, u32[]{:S(2)}, u32[]{:S(2)}) %collective-permute-start.5) | collective-permute-done | bytes 65568 | tf_op jit(solution)/shard_map/ppermute | solution.py:160
  346.4 3.7 collective-permute-start.12
  351.0 3.3 collective-permute-start.14
  354.7 2.1 collective-permute-done.14
  358.3 13.4 %gather_fusion.6 = bf16[2048,128]{1,0:T(8,128)(2,1)S(1)} fusion(bf16[16,16,16,128]{3,2,1,0:T(8,128)(2,1)S(1)} %gather_fusion.5, s32[2048]{0:T(1024)S(1)} %reshape.498), kind=kCustom, calls=%fused_computation.6 | custom fusion | bytes 1073152 | tf_op jit(solution)/shard_map/gather | solution.py:164
  371.9 9.5 %fusion.43 = f32[128,4096]{1,0:T(8,128)} fusion(bf16[128,2048]{1,0:T(8,128)(2,1)S(1)} %reshape.457, bf16[2048,4096]{1,0:T(8,128)(2,1)} %param.11), kind=kOutput, calls=%fused_computation.142 | convolution fusion | flops 2147483648 | bytes 19398656 | tf_op jit(solution)/shard_map/dot_general | solution.py:166
  381.4 33.4 %reduce-scatter.2.cloned.1.call-done = f32[128,2048]{1,0:T(8,128)} async-done(((f32[128,4096]{1,0:T(8,128)}), f32[128,2048]{1,0:T(8,128)}) %reduce-scatter.2.cloned.1.call-update) | async-done | bytes 1048592 | tf_op jit(solution)/shard_map/reduce_scatter | solution.py:167
  414.8 2.1 convert_element_type.19
  (192 shorter events, 55.7 us)
Async XLA Ops:
  10.3 25.9 %copy-start.2 = (bf16[128,2048]{1,0:T(8,128)(2,1)S(1)}, bf16[128,2048]{1,0:T(8,128)(2,1)}, u32[]{:S(2)}) copy-start(bf16[128,2048]{1,0:T(8,128)(2,1)} %param.7) | copy-start | bytes 1572868
  10.3 26.0 %copy-start.3 = (bf16[128,2048]{1,0:T(8,128)(2,1)S(1)}, bf16[128,2048]{1,0:T(8,128)(2,1)}, u32[]{:S(2)}) copy-start(bf16[128,2048]{1,0:T(8,128)(2,1)} %param.8) | copy-start | bytes 1572868
  80.4 7.6 %copy-start.1 = (s32[16,16,16]{2,1,0:T(8,128)S(1)}, s32[16,16,16]{2,1,0:T(8,128)}, u32[]{:S(2)}) copy-start(s32[16,16,16]{2,1,0:T(8,128)} %param.10) | copy-start | bytes 49156
  80.4 48.5 %all-to-all-start = ((bf16[16,16,16,256]{3,2,1,0:T(8,128)(2,1)}), bf16[16,16,16,256]{3,2,1,0:T(8,128)(2,1)S(1)}, u32[]{:S(2)}, u32[]{:S(2)}) async-start(bf16[16,16,16,256]{3,2,1,0:T(8,128)(2,1)} %broadcast_select_fusion.2), calls=%async_computation | async-start | bytes 4194304 | tf_op jit(solution)/shard_map/all_to_all | solution.py:123
  88.0 326.8 %reduce-scatter.2.cloned.1.call-start = ((), (), s32[]{:S(2)}) async-start(), calls=%async_computation.2 | async-start | bytes 3145728 | tf_op jit(solution)/shard_map/reduce_scatter | solution.py:167
  216.9 4.1 copy-start.4
  219.8 33.9 %collective-permute-start = (bf16[16,256,256]{2,1,0:T(8,128)(2,1)}, bf16[16,256,256]{2,1,0:T(8,128)(2,1)}, u32[]{:S(2)}, u32[]{:S(2)}) collective-permute-start(bf16[16,256,256]{2,1,0:T(8,128)(2,1)} %broadcast_select_fusion.1), channel_id=1, source_target_pairs={{0,2},{2,4},{4,6},{6,8},{8,10},{10,12},{12,14},{14,16},{16,18},{18... | collective-permute-start | bytes 6291464 | tf_op jit(solution)/shard_map/ppermute | solution.py:24
  221.3 2.0 copy-start
  327.5 6.5 %collective-permute-start.1 = (bf16[1,16,16,128]{3,2,1,0:T(8,128)(2,1)S(1)}, bf16[1,16,16,128]{3,2,1,0:T(8,128)(2,1)S(1)}, u32[]{:S(2)}, u32[]{:S(2)}) collective-permute-start(bf16[1,16,16,128]{3,2,1,0:T(8,128)(2,1)S(1)} %get-tuple-element.79), channel_id=1, source_target_pairs={{0,2},{2,4},{4,6},{6,8},{8,10},{10,12},{12,14},{14,16},{16,18},{18... | collective-permute-start | bytes 196616 | tf_op jit(solution)/shard_map/ppermute | solution.py:160
  327.5 7.7 %collective-permute-start.2 = (bf16[1,16,16,128]{3,2,1,0:T(8,128)(2,1)S(1)}, bf16[1,16,16,128]{3,2,1,0:T(8,128)(2,1)S(1)}, u32[]{:S(2)}, u32[]{:S(2)}) collective-permute-start(bf16[1,16,16,128]{3,2,1,0:T(8,128)(2,1)S(1)} %get-tuple-element.78), channel_id=1, source_target_pairs={{0,4},{2,6},{4,8},{6,10},{8,12},{10,14},{12,16},{14,18},{16,20},{1... | collective-permute-start | bytes 196616 | tf_op jit(solution)/shard_map/ppermute | solution.py:160
  327.6 9.4 %collective-permute-start.3 = (bf16[1,16,16,128]{3,2,1,0:T(8,128)(2,1)S(1)}, bf16[1,16,16,128]{3,2,1,0:T(8,128)(2,1)S(1)}, u32[]{:S(2)}, u32[]{:S(2)}) collective-permute-start(bf16[1,16,16,128]{3,2,1,0:T(8,128)(2,1)S(1)} %get-tuple-element.77), channel_id=1, source_target_pairs={{0,6},{2,8},{4,10},{6,12},{8,14},{10,16},{12,18},{14,20},{16,22},{... | collective-permute-start | bytes 196616 | tf_op jit(solution)/shard_map/ppermute | solution.py:160
  329.9 7.9 %collective-permute-start.4 = (bf16[1,16,16,128]{3,2,1,0:T(8,128)(2,1)S(1)}, bf16[1,16,16,128]{3,2,1,0:T(8,128)(2,1)S(1)}, u32[]{:S(2)}, u32[]{:S(2)}) collective-permute-start(bf16[1,16,16,128]{3,2,1,0:T(8,128)(2,1)S(1)} %get-tuple-element.76), channel_id=1, source_target_pairs={{0,8},{2,10},{4,12},{6,14},{8,16},{10,18},{12,20},{14,22},{16,24},... | collective-permute-start | bytes 196616 | tf_op jit(solution)/shard_map/ppermute | solution.py:160
  331.5 14.2 %collective-permute-start.5 = (bf16[1,16,16,128]{3,2,1,0:T(8,128)(2,1)S(1)}, bf16[1,16,16,128]{3,2,1,0:T(8,128)(2,1)S(1)}, u32[]{:S(2)}, u32[]{:S(2)}) collective-permute-start(bf16[1,16,16,128]{3,2,1,0:T(8,128)(2,1)S(1)} %get-tuple-element.75), channel_id=1, source_target_pairs={{0,10},{2,12},{4,14},{6,16},{8,18},{10,20},{12,22},{14,24},{16,26}... | collective-permute-start | bytes 196616 | tf_op jit(solution)/shard_map/ppermute | solution.py:160
  334.0 12.0 %collective-permute-start.6 = (bf16[1,16,16,128]{3,2,1,0:T(8,128)(2,1)S(1)}, bf16[1,16,16,128]{3,2,1,0:T(8,128)(2,1)S(1)}, u32[]{:S(2)}, u32[]{:S(2)}) collective-permute-start(bf16[1,16,16,128]{3,2,1,0:T(8,128)(2,1)S(1)} %get-tuple-element.74), channel_id=1, source_target_pairs={{0,12},{2,14},{4,16},{6,18},{8,20},{10,22},{12,24},{14,26},{16,28}... | collective-permute-start | bytes 196616 | tf_op jit(solution)/shard_map/ppermute | solution.py:160
  335.2 11.2 %collective-permute-start.7 = (bf16[1,16,16,128]{3,2,1,0:T(8,128)(2,1)S(1)}, bf16[1,16,16,128]{3,2,1,0:T(8,128)(2,1)S(1)}, u32[]{:S(2)}, u32[]{:S(2)}) collective-permute-start(bf16[1,16,16,128]{3,2,1,0:T(8,128)(2,1)S(1)} %get-tuple-element.73), channel_id=1, source_target_pairs={{0,14},{2,16},{4,18},{6,20},{8,22},{10,24},{12,26},{14,28},{16,30}... | collective-permute-start | bytes 196616 | tf_op jit(solution)/shard_map/ppermute | solution.py:160
  337.0 13.2 %collective-permute-start.8 = (bf16[1,16,16,128]{3,2,1,0:T(8,128)(2,1)S(1)}, bf16[1,16,16,128]{3,2,1,0:T(8,128)(2,1)S(1)}, u32[]{:S(2)}, u32[]{:S(2)}) collective-permute-start(bf16[1,16,16,128]{3,2,1,0:T(8,128)(2,1)S(1)} %get-tuple-element.72), channel_id=1, source_target_pairs={{0,16},{2,18},{4,20},{6,22},{8,24},{10,26},{12,28},{14,30},{16,0},... | collective-permute-start | bytes 196616 | tf_op jit(solution)/shard_map/ppermute | solution.py:160
  337.8 13.3 %collective-permute-start.9 = (bf16[1,16,16,128]{3,2,1,0:T(8,128)(2,1)S(1)}, bf16[1,16,16,128]{3,2,1,0:T(8,128)(2,1)S(1)}, u32[]{:S(2)}, u32[]{:S(2)}) collective-permute-start(bf16[1,16,16,128]{3,2,1,0:T(8,128)(2,1)S(1)} %get-tuple-element.71), channel_id=1, source_target_pairs={{0,18},{2,20},{4,22},{6,24},{8,26},{10,28},{12,30},{14,0},{16,2},{... | collective-permute-start | bytes 196616 | tf_op jit(solution)/shard_map/ppermute | solution.py:160
  345.7 8.6 %collective-permute-start.10 = (bf16[1,16,16,128]{3,2,1,0:T(8,128)(2,1)S(1)}, bf16[1,16,16,128]{3,2,1,0:T(8,128)(2,1)S(1)}, u32[]{:S(2)}, u32[]{:S(2)}) collective-permute-start(bf16[1,16,16,128]{3,2,1,0:T(8,128)(2,1)S(1)} %get-tuple-element.70), channel_id=1, source_target_pairs={{0,20},{2,22},{4,24},{6,26},{8,28},{10,30},{12,0},{14,2},{16,4},{1... | collective-permute-start | bytes 196616 | tf_op jit(solution)/shard_map/ppermute | solution.py:160
  345.9 8.7 %collective-permute-start.11 = (bf16[1,16,16,128]{3,2,1,0:T(8,128)(2,1)S(1)}, bf16[1,16,16,128]{3,2,1,0:T(8,128)(2,1)S(1)}, u32[]{:S(2)}, u32[]{:S(2)}) collective-permute-start(bf16[1,16,16,128]{3,2,1,0:T(8,128)(2,1)S(1)} %get-tuple-element.69), channel_id=1, source_target_pairs={{0,22},{2,24},{4,26},{6,28},{8,30},{10,0},{12,2},{14,4},{16,6},{18... | collective-permute-start | bytes 196616 | tf_op jit(solution)/shard_map/ppermute | solution.py:160
  346.4 8.2 %collective-permute-start.12 = (bf16[1,16,16,128]{3,2,1,0:T(8,128)(2,1)S(1)}, bf16[1,16,16,128]{3,2,1,0:T(8,128)(2,1)S(1)}, u32[]{:S(2)}, u32[]{:S(2)}) collective-permute-start(bf16[1,16,16,128]{3,2,1,0:T(8,128)(2,1)S(1)} %get-tuple-element.68), channel_id=1, source_target_pairs={{0,24},{2,26},{4,28},{6,30},{8,0},{10,2},{12,4},{14,6},{16,8},{18,... | collective-permute-start | bytes 196616 | tf_op jit(solution)/shard_map/ppermute | solution.py:160
  350.2 4.5 %collective-permute-start.13 = (bf16[1,16,16,128]{3,2,1,0:T(8,128)(2,1)S(1)}, bf16[1,16,16,128]{3,2,1,0:T(8,128)(2,1)S(1)}, u32[]{:S(2)}, u32[]{:S(2)}) collective-permute-start(bf16[1,16,16,128]{3,2,1,0:T(8,128)(2,1)S(1)} %get-tuple-element.67), channel_id=1, source_target_pairs={{0,26},{2,28},{4,30},{6,0},{8,2},{10,4},{12,6},{14,8},{16,10},{18,... | collective-permute-start | bytes 196616 | tf_op jit(solution)/shard_map/ppermute | solution.py:160
  351.0 5.8 %collective-permute-start.14 = (bf16[1,16,16,128]{3,2,1,0:T(8,128)(2,1)S(1)}, bf16[1,16,16,128]{3,2,1,0:T(8,128)(2,1)S(1)}, u32[]{:S(2)}, u32[]{:S(2)}) collective-permute-start(bf16[1,16,16,128]{3,2,1,0:T(8,128)(2,1)S(1)} %get-tuple-element.66), channel_id=1, source_target_pairs={{0,28},{2,30},{4,0},{6,2},{8,4},{10,6},{12,8},{14,10},{16,12},{18,... | collective-permute-start | bytes 196616 | tf_op jit(solution)/shard_map/ppermute | solution.py:160
  354.3 3.2 collective-permute-start.15
Sparse Core Ops, SparseCore 0:
  381.5 33.2 reduce-scatter.1
